TPU v7x, 512 devices: a whole 4x8x8 slice. The times are simulated.
512 devices in a mesh: energy: 128 (over z, y, core), transpor: 4 (over x).
Axes of the slice: x: 4, y: 8, z: 8, core: 2. Of those that a mesh axis runs over, the one named last changes fastest.
Arguments:
- onsite: float32 [4, 128, 128], P('transpor'), may hold values from -1 to 1, as said below
- hopping: float32 [4, 128, 128], P('transpor'), may hold values from -0.25 to 0.25
- selfenergy: float32 [128, 4, 128, 128], P('energy', 'transpor'), may hold values from -1 to 1, as said below
- broadening: float32 [128, 4, 128], P('energy', 'transpor'), may hold values from 0.1 to 0.5
Outputs:
- green: float32 [128, 2, 4, 128, 128], P('energy', None, 'transpor')
- polar: float32 [128, 2, 4, 128, 128], P('energy', None, 'transpor')
Inputs may be any that keep to these rules, and one draw needn't show every extreme that they name: `onsite`: each block is symmetric. `selfenergy`: each block is symmetric.
All inputs are finite; a program needn't handle non-finite values.
Results may differ from a plain program's by a relative error of at most 0.00021.
Values sent between devices are 32-bit elements; how exact they have to be, the bound alone decides.
A program may use at most 128 MiB of HBM per device.

v0:
```python
import math
import jax
import jax.numpy as jnp
from jax import lax
from jax.sharding import PartitionSpec as P

ENERGY_LOW = -1.5
ENERGY_HIGH = 1.5


def prefix_2(part, axis, combine, identity, reverse):
    count = lax.axis_size(axis)
    place = lax.axis_index(axis)
    ahead = count - 1 - place if reverse else place
    gathered = jax.tree.map(lambda a: lax.all_gather(a, axis), part)
    state = jax.tree.map(lambda a, e: jnp.zeros_like(a) + jnp.asarray(e, a.dtype), part, identity)

    def one(hop, state):
        source = count - 1 - hop if reverse else hop
        return combine(
            state, jax.tree.map(lambda a: lax.dynamic_index_in_dim(a, source, 0, False), gathered)
        )

    return lax.fori_loop(0, ahead, one, state)


def product(left, right):
    return jnp.matmul(left, right, precision=lax.Precision.HIGHEST)


def flipped(matrix):
    return jnp.swapaxes(matrix, -1, -2)


def complex_mul(first, second):
    return (
        product(first[0], second[0]) - product(first[1], second[1]),
        product(first[0], second[1]) + product(first[1], second[0]),
    )


def complex_add(first, second):
    return (first[0] + second[0], first[1] + second[1])


def complex_flip(value):
    return (flipped(value[0]), flipped(value[1]))


def real_left(matrix, value):
    return (product(matrix, value[0]), product(matrix, value[1]))


def real_right(value, matrix):
    return (product(value[0], matrix), product(value[1], matrix))


def invert(value):
    real_part, imag_part = value
    normal_real = product(flipped(real_part), real_part) + product(flipped(imag_part), imag_part)
    normal_imag = product(flipped(real_part), imag_part) - product(flipped(imag_part), real_part)
    upper_rows = jnp.concatenate([normal_real, -normal_imag], -1)
    lower_rows = jnp.concatenate([normal_imag, normal_real], -1)
    factor = jnp.linalg.cholesky(jnp.concatenate([upper_rows, lower_rows], -2))
    target = jnp.concatenate([flipped(real_part), -flipped(imag_part)], -2)
    solved = jax.scipy.linalg.cho_solve((factor, True), target)
    orders = real_part.shape[-1]
    return (solved[..., :orders, :], solved[..., orders:, :])


def joined(left, right, coupling):
    first_a, cross_a, last_a = left
    first_b, cross_b, last_b = right
    unit_matrix = jnp.eye(coupling.shape[-1], dtype=jnp.float32)
    dressing = real_right(real_left(coupling, first_b), flipped(coupling))
    loaded = complex_mul(last_a, dressing)
    kernel = invert((unit_matrix - loaded[0], -loaded[1]))
    weighted = complex_mul(kernel, last_a)
    first_new = complex_add(
        first_a,
        complex_mul(complex_mul(cross_a, complex_mul(dressing, kernel)), complex_flip(cross_a)),
    )
    bridge = real_left(coupling, cross_b)
    lifted = complex_add(cross_a, complex_mul(cross_a, complex_mul(dressing, weighted)))
    cross_new = complex_mul(lifted, bridge)
    last_new = complex_add(last_b, complex_mul(complex_flip(bridge), complex_mul(weighted, bridge)))
    return (first_new, cross_new, last_new)


def packed(corners, coupling, marker):
    return (
        corners[0][0],
        corners[0][1],
        corners[1][0],
        corners[1][1],
        corners[2][0],
        corners[2][1],
        coupling,
        marker,
    )


def unpacked(element):
    return ((element[0], element[1]), (element[2], element[3]), (element[4], element[5]))


def tree_join(earlier, later):
    merged = packed(
        joined(unpacked(earlier), unpacked(later), earlier[6]),
        later[6],
        jnp.maximum(earlier[7], later[7]),
    )
    has_early = earlier[7][0] > 0
    has_late = later[7][0] > 0
    return tuple(
        (
            jnp.where(has_early, jnp.where(has_late, whole_part, early_part), late_part)
            for whole_part, early_part, late_part in zip(merged, earlier, later)
        )
    )


def reverse_join(earlier, later):
    return tree_join(later, earlier)


def transform_sum(values):
    energy_total = values.shape[0]
    length = 2 * energy_total
    phase = (
        jnp.arange(length, dtype=jnp.int32)[:, None]
        * jnp.arange(energy_total, dtype=jnp.int32)[None, :]
        % length
    )
    angles = phase.astype(jnp.float32) * (2.0 * math.pi / length)
    cosine = jnp.cos(angles)
    sine_table = jnp.sin(angles)
    trailing = values.shape[2:]
    real_flat = values[:, 0].reshape(energy_total, -1)
    imag_flat = values[:, 1].reshape(energy_total, -1)
    spec_real = product(cosine, real_flat) + product(sine_table, imag_flat)
    spec_imag = product(cosine, imag_flat) - product(sine_table, real_flat)
    power = spec_real * spec_real + spec_imag * spec_imag
    real_sum = product(flipped(cosine), power) / (length * energy_total)
    imag_sum = product(flipped(sine_table), power) / (length * energy_total)
    return jnp.stack(
        [
            real_sum.reshape((energy_total,) + trailing),
            imag_sum.reshape((energy_total,) + trailing),
        ],
        1,
    )


def on_device(onsite, hopping, selfenergy, broadening):
    per_energy = selfenergy.shape[0]
    blocks = onsite.shape[0]
    orders = onsite.shape[-1]
    axis_span = lax.axis_size("transpor")
    energy_count = per_energy * lax.axis_size("energy")
    first_energy = lax.axis_index("energy") * per_energy
    levels = (
        ENERGY_LOW
        + (ENERGY_HIGH - ENERGY_LOW)
        * ((first_energy + jnp.arange(per_energy, dtype=jnp.int32)).astype(jnp.float32) + 0.5)
        / energy_count
    )
    unit_matrix = jnp.eye(orders, dtype=jnp.float32)
    outgoing = hopping[blocks - 1]
    at_end = (lax.axis_index("transpor") == axis_span - 1).astype(jnp.float32)
    contact = at_end * product(outgoing, flipped(outgoing))
    block_index = 0
    real_part = (
        levels[:, None, None] * unit_matrix - onsite[block_index] - selfenergy[:, block_index]
    )
    imag_part = broadening[:, block_index, :, None] * unit_matrix
    imag_part = imag_part + contact
    matrices = [(real_part, imag_part)]
    singles = [invert(matrix) for matrix in matrices]
    segment = (singles[0], singles[0], singles[0])
    element = packed(segment, outgoing, jnp.ones((1,), jnp.float32))
    neutral = tuple((jnp.zeros_like(member) for member in element))
    prefix = prefix_2(element, "transpor", tree_join, neutral, False)
    suffix = prefix_2(element, "transpor", reverse_join, neutral, True)
    sigma_left = real_right(real_left(flipped(prefix[6]), (prefix[4], prefix[5])), prefix[6])
    sigma_right = real_right(real_left(outgoing, (suffix[0], suffix[1])), flipped(outgoing))
    block_index = 0
    real_part, imag_part = matrices[block_index]
    real_part = real_part - sigma_left[0]
    imag_part = imag_part - sigma_left[1]
    real_part = real_part - sigma_right[0]
    imag_part = imag_part - sigma_right[1]
    connected = [invert((real_part, imag_part))]
    greens = [connected[-1]]
    green = jnp.stack(
        [
            jnp.stack([value_pair[0] for value_pair in greens], 1),
            jnp.stack([value_pair[1] for value_pair in greens], 1),
        ],
        1,
    )
    flattened = green.reshape(per_energy, 2, blocks, orders * orders)
    correlated = transform_sum(
        lax.all_to_all(flattened, "energy", split_axis=3, concat_axis=0, tiled=True)
    )
    returned = lax.all_to_all(correlated, "energy", split_axis=0, concat_axis=3, tiled=True)
    polar = returned.reshape(per_energy, 2, blocks, orders, orders)
    return (green, polar)


def solution(mesh):
    placed = (
        P("transpor", None, None),
        P("transpor", None, None),
        P("energy", "transpor", None, None),
        P("energy", "transpor", None),
    )
    return jax.shard_map(
        on_device,
        mesh=mesh,
        in_specs=placed,
        out_specs=(
            P("energy", None, "transpor", None, None),
            P("energy", None, "transpor", None, None),
        ),
        check_vma=False,
    )
```

profile of v0, /device:TPU:1, one launch (start us, length us, event | category | flops | bytes accessed | tf_op | source)
XLA Modules:
  0.0 622.7 jit_solution(16338300515268233573)
XLA Ops:
  5.0 11.7 %custom-call.41 = f32[1,128,128]{2,1,0:T(8,128)S(1)} custom-call(f32[1,128,128]{2,1,0:T(8,128)S(1)} %slice.245), custom_call_target="Cholesky" | custom-call | tf_op jit(solution)/shard_map/jit(cholesky)/cholesky/custom-call.2 | solution.py:64
  16.8 9.8 %custom-call.42 = f32[1,1,128,128]{2,3,1,0:T(8,128)S(1)} custom-call(f32[1,1,128,128]{3,2,1,0:T(8,128)S(1)} %get-tuple-element.618), custom_call_target="InvertDiagBlocksLowerTriangular" | custom-call | tf_op jit(solution)/shard_map/jit(cholesky)/cholesky/custom-call.5 | solution.py:64
  27.3 10.7 %all_gather.17 = f32[4,128,128]{2,1,0:T(8,128)S(1)} all-gather(f32[1,128,128]{2,1,0:T(8,128)} %param.14), channel_id=1, replica_groups=mesh['energy'=128,'transpor'=4] {'transpor'}, dimensions={0}, use_global_device_ids=true | all-gather | bytes 327680 | tf_op jit(solution)/shard_map/all_gather | solution.py:15
  40.0 8.3 %all-reduce.1 = f32[4]{0:T(128)S(1)} all-reduce(f32[4]{0:T(128)S(1)} %dynamic-update-slice.23), channel_id=1, replica_groups=mesh['energy'=128,'transpor'=4] {'transpor'}, use_global_device_ids=true, to_apply=%add.1 | all-reduce | flops 4 | bytes 32
  48.2 11.7 %custom-call.43 = f32[1,128,128]{2,1,0:T(8,128)S(1)} custom-call(f32[1,128,128]{2,1,0:T(8,128)S(1)} %fusion.147), custom_call_target="Cholesky" | custom-call | tf_op jit(solution)/shard_map/jit(cholesky)/cholesky/custom-call.3 | solution.py:64
  62.1 3.9 while.67
  62.7 1.3 bitcast_dynamic-update-slice_fusion.16
  64.7 1.3 bitcast_dynamic-update-slice_fusion.16
  66.1 19.7 %custom-call.45 = f32[2,128,128]{1,2,0:T(8,128)S(1)} custom-call(f32[2,128,128]{2,1,0:T(8,128)S(1)} %get-tuple-element.401), custom_call_target="InvertDiagBlocksLowerTriangular" | custom-call | tf_op jit(solution)/shard_map/jit(_cho_solve)/triangular_solve/custom-call.4 | solution.py:66
  87.3 9.4 %all-gather = f32[4,128,128]{2,1,0:T(8,128)S(1)} all-gather(f32[1,128,128]{2,1,0:T(8,128)S(1)} %get-tuple-element.610), channel_id=2, replica_groups=mesh['energy'=128,'transpor'=4] {'transpor'}, dimensions={0}, use_global_device_ids=true | all-gather | bytes 327680 | tf_op jit(solution)/shard_map/all_gather | solution.py:15
  96.7 9.8 %all-gather.1 = f32[4,128,128]{2,1,0:T(8,128)S(1)} all-gather(f32[1,128,128]{2,1,0:T(8,128)S(1)} %get-tuple-element.609), channel_id=3, replica_groups=mesh['energy'=128,'transpor'=4] {'transpor'}, dimensions={0}, use_global_device_ids=true | all-gather | bytes 327680 | tf_op jit(solution)/shard_map/all_gather | solution.py:15
  106.5 12.2 %while.64 = (s32[]{:T(128)}, f32[1,128,128]{2,1,0:T(8,128)S(1)}, f32[1,128,128]{2,1,0:T(8,128)S(1)}, f32[128,128]{1,0:T(8,128)S(1)}, f32[1]{0:T(128)}, /*index=5...) while((s32[]{:T(128)}, f32[1,128,128]{2,1,0:T(8,128)S(1)}, ...), condition=%wide.region_5.9_spmd, body=%wide.region_4.8_spmd.sunk | while | flops 806813952 | bytes 11471332 | solution.py:24
  119.3 214.8 %while.66 = (s32[]{:T(128)}, f32[1,128,128]{2,1,0:T(8,128)S(1)}, f32[1,128,128]{2,1,0:T(8,128)S(1)}, f32[1]{0:T(128)}, s32[]{:T(128)}, /*index=5*/f32[4,1]{0,1:T...) while((s32[]{:T(128)}, f32[1,128,128]{2,1,0:T(8,128)S(1)}, ...), condition=%wide.region_7.11_spmd, body=%wide.region_6.10_spmd.sunk | while | flops 806764800 | bytes 11342354 | solution.py:24
  122.9 11.7 %custom-call.68 = f32[1,128,128]{2,1,0:T(8,128)S(1)} custom-call(f32[1,128,128]{2,1,0:T(8,128)S(1)} %slice.430), custom_call_target="Cholesky" | custom-call | tf_op jit(solution)/shard_map/while/body/jit(cholesky)/cholesky/custom-call.2 | solution.py:64
  134.6 9.8 %custom-call.69 = f32[1,1,128,128]{2,3,1,0:T(8,128)S(1)} custom-call(f32[1,1,128,128]{3,2,1,0:T(8,128)S(1)} %get-tuple-element.883), custom_call_target="InvertDiagBlocksLowerTriangular" | custom-call | tf_op jit(solution)/shard_map/while/body/jit(cholesky)/cholesky/custom-call.5 | solution.py:64
  145.0 11.7 %custom-call.70 = f32[1,128,128]{2,1,0:T(8,128)S(1)} custom-call(f32[1,128,128]{2,1,0:T(8,128)S(1)} %fusion.661), custom_call_target="Cholesky" | custom-call | tf_op jit(solution)/shard_map/while/body/jit(cholesky)/cholesky/custom-call.3 | solution.py:64
  159.0 4.0 while.70
  159.6 1.3 bitcast_dynamic-update-slice_fusion.18
  161.6 1.3 bitcast_dynamic-update-slice_fusion.18
  163.0 19.7 %custom-call.72 = f32[2,128,128]{1,2,0:T(8,128)S(1)} custom-call(f32[2,128,128]{2,1,0:T(8,128)S(1)} %get-tuple-element.889), custom_call_target="InvertDiagBlocksLowerTriangular" | custom-call | tf_op jit(solution)/shard_map/while/body/jit(_cho_solve)/triangular_solve/custom-call.4 | solution.py:66
  194.3 11.7 %custom-call.68 = f32[1,128,128]{2,1,0:T(8,128)S(1)} custom-call(f32[1,128,128]{2,1,0:T(8,128)S(1)} %slice.430), custom_call_target="Cholesky" | custom-call | tf_op jit(solution)/shard_map/while/body/jit(cholesky)/cholesky/custom-call.2 | solution.py:64
  206.1 9.8 %custom-call.69 = f32[1,1,128,128]{2,3,1,0:T(8,128)S(1)} custom-call(f32[1,1,128,128]{3,2,1,0:T(8,128)S(1)} %get-tuple-element.883), custom_call_target="InvertDiagBlocksLowerTriangular" | custom-call | tf_op jit(solution)/shard_map/while/body/jit(cholesky)/cholesky/custom-call.5 | solution.py:64
  216.5 11.7 %custom-call.70 = f32[1,128,128]{2,1,0:T(8,128)S(1)} custom-call(f32[1,128,128]{2,1,0:T(8,128)S(1)} %fusion.661), custom_call_target="Cholesky" | custom-call | tf_op jit(solution)/shard_map/while/body/jit(cholesky)/cholesky/custom-call.3 | solution.py:64
  230.4 4.0 while.70
  231.1 1.3 bitcast_dynamic-update-slice_fusion.18
  234.4 19.7 %custom-call.72 = f32[2,128,128]{1,2,0:T(8,128)S(1)} custom-call(f32[2,128,128]{2,1,0:T(8,128)S(1)} %get-tuple-element.889), custom_call_target="InvertDiagBlocksLowerTriangular" | custom-call | tf_op jit(solution)/shard_map/while/body/jit(_cho_solve)/triangular_solve/custom-call.4 | solution.py:66
  265.8 11.7 %custom-call.68 = f32[1,128,128]{2,1,0:T(8,128)S(1)} custom-call(f32[1,128,128]{2,1,0:T(8,128)S(1)} %slice.430), custom_call_target="Cholesky" | custom-call | tf_op jit(solution)/shard_map/while/body/jit(cholesky)/cholesky/custom-call.2 | solution.py:64
  277.5 9.8 %custom-call.69 = f32[1,1,128,128]{2,3,1,0:T(8,128)S(1)} custom-call(f32[1,1,128,128]{3,2,1,0:T(8,128)S(1)} %get-tuple-element.883), custom_call_target="InvertDiagBlocksLowerTriangular" | custom-call | tf_op jit(solution)/shard_map/while/body/jit(cholesky)/cholesky/custom-call.5 | solution.py:64
  287.9 11.7 %custom-call.70 = f32[1,128,128]{2,1,0:T(8,128)S(1)} custom-call(f32[1,128,128]{2,1,0:T(8,128)S(1)} %fusion.661), custom_call_target="Cholesky" | custom-call | tf_op jit(solution)/shard_map/while/body/jit(cholesky)/cholesky/custom-call.3 | solution.py:64
  301.9 4.0 while.70
  305.9 19.7 %custom-call.72 = f32[2,128,128]{1,2,0:T(8,128)S(1)} custom-call(f32[2,128,128]{2,1,0:T(8,128)S(1)} %get-tuple-element.889), custom_call_target="InvertDiagBlocksLowerTriangular" | custom-call | tf_op jit(solution)/shard_map/while/body/jit(_cho_solve)/triangular_solve/custom-call.4 | solution.py:66
  337.0 11.7 %custom-call.46 = f32[1,128,128]{2,1,0:T(8,128)S(1)} custom-call(f32[1,128,128]{2,1,0:T(8,128)S(1)} %slice.255), custom_call_target="Cholesky" | custom-call | tf_op jit(solution)/shard_map/jit(cholesky)/cholesky/custom-call.2 | solution.py:64
  348.8 9.8 %custom-call.47 = f32[1,1,128,128]{2,3,1,0:T(8,128)S(1)} custom-call(f32[1,1,128,128]{3,2,1,0:T(8,128)S(1)} %get-tuple-element.614), custom_call_target="InvertDiagBlocksLowerTriangular" | custom-call | tf_op jit(solution)/shard_map/jit(cholesky)/cholesky/custom-call.5 | solution.py:64
  359.3 11.7 %custom-call.48 = f32[1,128,128]{2,1,0:T(8,128)S(1)} custom-call(f32[1,128,128]{2,1,0:T(8,128)S(1)} %fusion.150), custom_call_target="Cholesky" | custom-call | tf_op jit(solution)/shard_map/jit(cholesky)/cholesky/custom-call.3 | solution.py:64
  373.8 4.3 while.68
  374.6 1.4 bitcast_dynamic-update-slice_fusion.17
  376.7 1.4 bitcast_dynamic-update-slice_fusion.17
  378.1 19.7 %custom-call.50 = f32[2,128,128]{1,2,0:T(8,128)S(1)} custom-call(f32[2,128,128]{2,1,0:T(8,128)S(1)} %get-tuple-element.403), custom_call_target="InvertDiagBlocksLowerTriangular" | custom-call | tf_op jit(solution)/shard_map/jit(_cho_solve)/triangular_solve/custom-call.4 | solution.py:66
  399.4 12.1 %copy.118 = f32[1,1,1,16384]{1,2,0,3:T(1,128)} copy(f32[1,1,1,16384]{3,2,1,0:T(1,128)S(1)} %bitcast.935) | data formatting | bytes 131072 | tf_op jit(solution)/shard_map/stack | solution.py:195
  411.4 11.9 %copy.117 = f32[1,1,1,16384]{1,2,0,3:T(1,128)} copy(f32[1,1,1,16384]{3,2,1,0:T(1,128)S(1)} %bitcast.934) | data formatting | bytes 131072 | tf_op jit(solution)/shard_map/stack | solution.py:195
  423.4 20.7 %fusion.252 = f32[16384,1,1,2]{3,2,1,0:T(1,128)} fusion(f32[1,1,1,16384]{1,2,0,3:T(1,128)} %copy.118, f32[1,1,1,16384]{1,2,0,3:T(1,128)} %copy.117), kind=kLoop, calls=%fused_computation.405 | loop fusion | flops 32768 | bytes 262144
  444.6 74.5 %reduce.94 = f32[16384,2]{1,0:T(8,128)} reduce(f32[16384,1,1,2]{3,2,1,0:T(1,128)} %fusion.252, f32[]{:T(128)} %broadcast.260), dimensions={1,2}, to_apply=%fusion.252.reduce_sub_computation | reduce | bytes 262148
  519.0 7.6 %reshape.504 = f32[128,1,256]{2,1,0:T(1,128)S(1)} reshape(f32[16384,2]{1,0:T(8,128)} %reduce.94) | data formatting | bytes 262144
  526.6 40.4 %all_to_all.33 = f32[128,1,256]{2,1,0:T(1,128)S(1)} all-to-all(f32[128,1,256]{2,1,0:T(1,128)S(1)} %reshape.504), channel_id=1, replica_groups=mesh['energy'=128,'transpor'=4] {'energy'}, dimensions={0} | all-to-all | bytes 262144 | tf_op jit(solution)/shard_map/all_to_all | solution.py:204
  568.0 14.9 %reshape.505 = f32[16384,1,1,2]{3,2,1,0:T(1,128)} reshape(f32[128,256]{1,0:T(8,128)S(1)} %reduce.95) | data formatting | bytes 262144
  582.9 15.0 %copy.119 = f32[1,2,1,16384]{3,2,1,0:T(1,128)S(1)} copy(f32[1,2,1,16384]{1,2,0,3:T(1,128)} %bitcast.922) | data formatting | bytes 262144 | tf_op jit(solution)/shard_map/all_to_all | solution.py:204
  603.4 5.6 all-to-all-start.1
  609.7 12.2 %all-to-all-done.1 = f32[128,2,1,128]{3,2,1,0:T(1,128)S(1)} async-done(((f32[128,2,1,128]{3,2,1,0:T(1,128)}), f32[128,2,1,128]{3,2,1,0:T(1,128)S(1)}, u32[]{:S(2)}, u32[]{:S(2)}) %all-to-all-start.1) | async-done | bytes 131104 | tf_op jit(solution)/shard_map/all_to_all | solution.py:206
  (266 shorter events, 68.4 us)
Async XLA Ops:
  119.3 214.8 %copy-start = (f32[1,128,128]{2,1,0:T(8,128)S(1)}, f32[1,128,128]{2,1,0:T(8,128)}, u32[]{:S(2)}) copy-start(f32[1,128,128]{2,1,0:T(8,128)} %param.14) | copy-start | bytes 196612
  603.4 18.4 %all-to-all-start.1 = ((f32[128,2,1,128]{3,2,1,0:T(1,128)}), f32[128,2,1,128]{3,2,1,0:T(1,128)S(1)}, u32[]{:S(2)}, u32[]{:S(2)}) async-start(f32[128,2,1,128]{3,2,1,0:T(1,128)} %copy.120), calls=%async_computation.1 | async-start | bytes 262144 | tf_op jit(solution)/shard_map/all_to_all | solution.py:206
where the time goes:
time: 630 us; the launch traced here: 623 us
  other arithmetic  368 us (58%)
  local copies, waits for them, and re-layouts  88.7 us (14%)
  blocking collectives  78.6 us (12%)
  matrix products  42 us (7%)
  loops' own time  23.3 us (4%)
  waiting for transfers between devices  12.2 us (2%)
    another operation x31, other arithmetic, invert(): factor = jnp.linalg.cholesky(jnp.concatenate([upper_rows, lower_rows], -2))  171 us
    another operation x17, other arithmetic, invert(): solved = jax.scipy.linalg.cho_solve((factor, True), target)  98.5 us
    unnamed x2, other arithmetic  95.1 us
    all_to_all x1, blocking collectives, on_device(): lax.all_to_all(flattened, 'energy', split_axis=3, concat_axis=0, tiled=True)  40.4 us
    dot_general x95, matrix products, product(): return jnp.matmul(left, right, precision=lax.Precision.HIGHEST)  31.8 us
    all_gather x3, blocking collectives, prefix_2(): gathered = jax.tree.map(lambda a: lax.all_gather(a, axis), part)  29.9 us
    unnamed x11, local copies, waits for them, and re-layouts  27.5 us
    another operation x2, local copies, waits for them, and re-layouts, on_device(): jnp.stack([jnp.stack([value_pair[0] for value_pair in greens], 1), jnp.st...  24 us
  transfers between devices with their start and end apart: 1, of which 1 were waited for; matrix products, arithmetic and copies ran while one was open for 0% of the time, Pallas kernels for 0%

commit v1 on v0

--- a/solution.py
+++ b/solution.py
@@ -201,7 +201,12 @@
     )
     flattened = green.reshape(per_energy, 2, blocks, orders * orders)
     correlated = transform_sum(
-        lax.all_to_all(flattened, "energy", split_axis=3, concat_axis=0, tiled=True)
+        jnp.concatenate(
+            lax.all_to_all(
+                jnp.stack(jnp.split(flattened, lax.axis_size("energy"), axis=3)), "energy", 0, 0
+            ),
+            axis=0,
+        )
     )
     returned = lax.all_to_all(correlated, "energy", split_axis=0, concat_axis=3, tiled=True)
     polar = returned.reshape(per_energy, 2, blocks, orders, orders)

time: 630 us -> 472 us (0.75)
  other arithmetic: 368 us -> 272 us
  local copies, waits for them, and re-layouts: 88.7 us -> 27.8 us
    unnamed x2 -> x0, other arithmetic: 95.1 us -> none
    another operation x6 -> x5, local copies, waits for them, and re-layouts: 24 us -> 0.03 us  [the longest x2 24 us: on_device(): jnp.stack([jnp.stack([value_pair[0] for value_pair in greens], 1), jnp.st...]
    unnamed x11 -> x139, local copies, waits for them, and re-layouts: 27.5 us -> 5.43 us
    all_to_all x1 -> x0, local copies, waits for them, and re-layouts: 15 us -> none  [on_device(): lax.all_to_all(flattened, 'energy', split_axis=3, concat_axis=0, tiled=True)]
where the time goes in v1:
time: 472 us; the launch traced here: 465 us
  other arithmetic  272 us (58%)
  blocking collectives  78.7 us (17%)
  matrix products  41.1 us (9%)
  local copies, waits for them, and re-layouts  27.8 us (6%)
  loops' own time  23 us (5%)
  waiting for transfers between devices  12.2 us (3%)
  starting transfers between devices  5.56 us (1%)
    another operation x31, other arithmetic, invert(): factor = jnp.linalg.cholesky(jnp.concatenate([upper_rows, lower_rows], -2))  171 us
    another operation x17, other arithmetic, invert(): solved = jax.scipy.linalg.cho_solve((factor, True), target)  98.5 us
    all_to_all x1, blocking collectives, on_device(): lax.all_to_all(jnp.stack(jnp.split(flattened, lax.axis_size('energy'), ax...  40.3 us
    dot_general x95, matrix products, product(): return jnp.matmul(left, right, precision=lax.Precision.HIGHEST)  30.9 us
    all_gather x3, blocking collectives, prefix_2(): gathered = jax.tree.map(lambda a: lax.all_gather(a, axis), part)  29.8 us
    another operation x2, loops' own time, prefix_2(): return lax.fori_loop(0, ahead, one, state)  22.6 us
    another operation x36, local copies, waits for them, and re-layouts, invert(): solved = jax.scipy.linalg.cho_solve((factor, True), target)  20.2 us
    all_to_all x1, waiting for transfers between devices, on_device(): lax.all_to_all(correlated, 'energy', split_axis=0, concat_axis=3, tiled=T...  12.2 us
  transfers between devices with their start and end apart: 1, of which 1 were waited for; matrix products, arithmetic and copies ran while one was open for 0% of the time, Pallas kernels for 0%

profile of v1, /device:TPU:1, one launch (start us, length us, event | category | flops | bytes accessed | tf_op | source)
XLA Modules:
  0.0 465.3 jit_solution(10801398621108489814)
XLA Ops:
  0.7 1.0 copy.158
  4.0 11.7 %custom-call.41 = f32[1,128,128]{2,1,0:T(8,128)S(1)} custom-call(f32[1,128,128]{2,1,0:T(8,128)S(1)} %slice.245), custom_call_target="Cholesky" | custom-call | tf_op jit(solution)/shard_map/jit(cholesky)/cholesky/custom-call.2 | solution.py:64
  15.8 9.8 %custom-call.42 = f32[1,1,128,128]{2,3,1,0:T(8,128)S(1)} custom-call(f32[1,1,128,128]{3,2,1,0:T(8,128)S(1)} %get-tuple-element.683), custom_call_target="InvertDiagBlocksLowerTriangular" | custom-call | tf_op jit(solution)/shard_map/jit(cholesky)/cholesky/custom-call.5 | solution.py:64
  26.3 10.5 %all_gather.17 = f32[4,128,128]{2,1,0:T(8,128)S(1)} all-gather(f32[1,128,128]{2,1,0:T(8,128)S(1)} %copy-done), channel_id=1, replica_groups=mesh['energy'=128,'transpor'=4] {'transpor'}, dimensions={0}, use_global_device_ids=true | all-gather | bytes 327680 | tf_op jit(solution)/shard_map/all_gather | solution.py:15
  36.8 1.3 dynamic-slice.18
  38.7 8.6 %all-reduce.1 = f32[4]{0:T(128)S(1)} all-reduce(f32[4]{0:T(128)S(1)} %dynamic-update-slice.23), channel_id=1, replica_groups=mesh['energy'=128,'transpor'=4] {'transpor'}, use_global_device_ids=true, to_apply=%add.1 | all-reduce | flops 4 | bytes 32
  47.3 11.7 %custom-call.43 = f32[1,128,128]{2,1,0:T(8,128)S(1)} custom-call(f32[1,128,128]{2,1,0:T(8,128)S(1)} %fusion.147), custom_call_target="Cholesky" | custom-call | tf_op jit(solution)/shard_map/jit(cholesky)/cholesky/custom-call.3 | solution.py:64
  61.2 3.9 while.67
  61.8 1.3 bitcast_dynamic-update-slice_fusion.16
  63.8 1.3 bitcast_dynamic-update-slice_fusion.16
  65.1 19.7 %custom-call.45 = f32[2,128,128]{1,2,0:T(8,128)S(1)} custom-call(f32[2,128,128]{2,1,0:T(8,128)S(1)} %get-tuple-element.401), custom_call_target="InvertDiagBlocksLowerTriangular" | custom-call | tf_op jit(solution)/shard_map/jit(_cho_solve)/triangular_solve/custom-call.4 | solution.py:66
  86.4 9.4 %all-gather = f32[4,128,128]{2,1,0:T(8,128)S(1)} all-gather(f32[1,128,128]{2,1,0:T(8,128)S(1)} %get-tuple-element.675), channel_id=2, replica_groups=mesh['energy'=128,'transpor'=4] {'transpor'}, dimensions={0}, use_global_device_ids=true | all-gather | bytes 327680 | tf_op jit(solution)/shard_map/all_gather | solution.py:15
  95.7 9.8 %all-gather.1 = f32[4,128,128]{2,1,0:T(8,128)S(1)} all-gather(f32[1,128,128]{2,1,0:T(8,128)S(1)} %get-tuple-element.674), channel_id=3, replica_groups=mesh['energy'=128,'transpor'=4] {'transpor'}, dimensions={0}, use_global_device_ids=true | all-gather | bytes 327680 | tf_op jit(solution)/shard_map/all_gather | solution.py:15
  105.6 12.2 %while.64 = (s32[]{:T(128)}, f32[1,128,128]{2,1,0:T(8,128)S(1)}, f32[1,128,128]{2,1,0:T(8,128)S(1)}, f32[128,128]{1,0:T(8,128)S(1)}, f32[1]{0:T(128)}, /*index=5...) while((s32[]{:T(128)}, f32[1,128,128]{2,1,0:T(8,128)S(1)}, ...), condition=%wide.region_5.9_spmd, body=%wide.region_4.8_spmd.sunk | while | flops 806813952 | bytes 11471332 | solution.py:24
  118.4 214.5 %while.66 = (s32[]{:T(128)}, f32[1,128,128]{2,1,0:T(8,128)S(1)}, f32[1,128,128]{2,1,0:T(8,128)S(1)}, f32[1]{0:T(128)}, s32[]{:T(128)}, /*index=5*/f32[4,1]{0,1:T...) while((s32[]{:T(128)}, f32[1,128,128]{2,1,0:T(8,128)S(1)}, ...), condition=%wide.region_7.11_spmd, body=%wide.region_6.10_spmd.sunk | while | flops 806764800 | bytes 11342354 | solution.py:24
  121.9 11.7 %custom-call.70 = f32[1,128,128]{2,1,0:T(8,128)S(1)} custom-call(f32[1,128,128]{2,1,0:T(8,128)S(1)} %slice.426), custom_call_target="Cholesky" | custom-call | tf_op jit(solution)/shard_map/while/body/jit(cholesky)/cholesky/custom-call.2 | solution.py:64
  133.6 9.8 %custom-call.71 = f32[1,1,128,128]{2,3,1,0:T(8,128)S(1)} custom-call(f32[1,1,128,128]{3,2,1,0:T(8,128)S(1)} %get-tuple-element.948), custom_call_target="InvertDiagBlocksLowerTriangular" | custom-call | tf_op jit(solution)/shard_map/while/body/jit(cholesky)/cholesky/custom-call.5 | solution.py:64
  144.0 11.7 %custom-call.72 = f32[1,128,128]{2,1,0:T(8,128)S(1)} custom-call(f32[1,128,128]{2,1,0:T(8,128)S(1)} %fusion.665), custom_call_target="Cholesky" | custom-call | tf_op jit(solution)/shard_map/while/body/jit(cholesky)/cholesky/custom-call.3 | solution.py:64
  158.0 4.0 while.70
  158.6 1.3 bitcast_dynamic-update-slice_fusion.18
  160.7 1.3 bitcast_dynamic-update-slice_fusion.18
  162.0 19.7 %custom-call.74 = f32[2,128,128]{1,2,0:T(8,128)S(1)} custom-call(f32[2,128,128]{2,1,0:T(8,128)S(1)} %get-tuple-element.954), custom_call_target="InvertDiagBlocksLowerTriangular" | custom-call | tf_op jit(solution)/shard_map/while/body/jit(_cho_solve)/triangular_solve/custom-call.4 | solution.py:66
  187.0 0.9 fusion.678
  193.3 11.7 %custom-call.70 = f32[1,128,128]{2,1,0:T(8,128)S(1)} custom-call(f32[1,128,128]{2,1,0:T(8,128)S(1)} %slice.426), custom_call_target="Cholesky" | custom-call | tf_op jit(solution)/shard_map/while/body/jit(cholesky)/cholesky/custom-call.2 | solution.py:64
  205.1 9.8 %custom-call.71 = f32[1,1,128,128]{2,3,1,0:T(8,128)S(1)} custom-call(f32[1,1,128,128]{3,2,1,0:T(8,128)S(1)} %get-tuple-element.948), custom_call_target="InvertDiagBlocksLowerTriangular" | custom-call | tf_op jit(solution)/shard_map/while/body/jit(cholesky)/cholesky/custom-call.5 | solution.py:64
  215.5 11.7 %custom-call.72 = f32[1,128,128]{2,1,0:T(8,128)S(1)} custom-call(f32[1,128,128]{2,1,0:T(8,128)S(1)} %fusion.665), custom_call_target="Cholesky" | custom-call | tf_op jit(solution)/shard_map/while/body/jit(cholesky)/cholesky/custom-call.3 | solution.py:64
  229.4 4.0 while.70
  230.1 1.3 bitcast_dynamic-update-slice_fusion.18
  232.1 1.3 bitcast_dynamic-update-slice_fusion.18
  233.5 19.7 %custom-call.74 = f32[2,128,128]{1,2,0:T(8,128)S(1)} custom-call(f32[2,128,128]{2,1,0:T(8,128)S(1)} %get-tuple-element.954), custom_call_target="InvertDiagBlocksLowerTriangular" | custom-call | tf_op jit(solution)/shard_map/while/body/jit(_cho_solve)/triangular_solve/custom-call.4 | solution.py:66
  264.8 11.7 %custom-call.70 = f32[1,128,128]{2,1,0:T(8,128)S(1)} custom-call(f32[1,128,128]{2,1,0:T(8,128)S(1)} %slice.426), custom_call_target="Cholesky" | custom-call | tf_op jit(solution)/shard_map/while/body/jit(cholesky)/cholesky/custom-call.2 | solution.py:64
  276.5 9.8 %custom-call.71 = f32[1,1,128,128]{2,3,1,0:T(8,128)S(1)} custom-call(f32[1,1,128,128]{3,2,1,0:T(8,128)S(1)} %get-tuple-element.948), custom_call_target="InvertDiagBlocksLowerTriangular" | custom-call | tf_op jit(solution)/shard_map/while/body/jit(cholesky)/cholesky/custom-call.5 | solution.py:64
  286.9 11.7 %custom-call.72 = f32[1,128,128]{2,1,0:T(8,128)S(1)} custom-call(f32[1,128,128]{2,1,0:T(8,128)S(1)} %fusion.665), custom_call_target="Cholesky" | custom-call | tf_op jit(solution)/shard_map/while/body/jit(cholesky)/cholesky/custom-call.3 | solution.py:64
  300.9 4.0 while.70
  301.5 1.3 bitcast_dynamic-update-slice_fusion.18
  303.6 1.3 bitcast_dynamic-update-slice_fusion.18
  304.9 19.7 %custom-call.74 = f32[2,128,128]{1,2,0:T(8,128)S(1)} custom-call(f32[2,128,128]{2,1,0:T(8,128)S(1)} %get-tuple-element.954), custom_call_target="InvertDiagBlocksLowerTriangular" | custom-call | tf_op jit(solution)/shard_map/while/body/jit(_cho_solve)/triangular_solve/custom-call.4 | solution.py:66
  330.0 0.9 fusion.678
  335.8 11.7 %custom-call.46 = f32[1,128,128]{2,1,0:T(8,128)S(1)} custom-call(f32[1,128,128]{2,1,0:T(8,128)S(1)} %slice.255), custom_call_target="Cholesky" | custom-call | tf_op jit(solution)/shard_map/jit(cholesky)/cholesky/custom-call.2 | solution.py:64
  347.6 9.8 %custom-call.47 = f32[1,1,128,128]{2,3,1,0:T(8,128)S(1)} custom-call(f32[1,1,128,128]{3,2,1,0:T(8,128)S(1)} %get-tuple-element.679), custom_call_target="InvertDiagBlocksLowerTriangular" | custom-call | tf_op jit(solution)/shard_map/jit(cholesky)/cholesky/custom-call.5 | solution.py:64
  358.1 11.7 %custom-call.48 = f32[1,128,128]{2,1,0:T(8,128)S(1)} custom-call(f32[1,128,128]{2,1,0:T(8,128)S(1)} %fusion.150), custom_call_target="Cholesky" | custom-call | tf_op jit(solution)/shard_map/jit(cholesky)/cholesky/custom-call.3 | solution.py:64
  372.6 4.3 while.68
  373.4 1.4 bitcast_dynamic-update-slice_fusion.17
  375.5 1.4 bitcast_dynamic-update-slice_fusion.17
  376.9 19.7 %custom-call.50 = f32[2,128,128]{1,2,0:T(8,128)S(1)} custom-call(f32[2,128,128]{2,1,0:T(8,128)S(1)} %get-tuple-element.403), custom_call_target="InvertDiagBlocksLowerTriangular" | custom-call | tf_op jit(solution)/shard_map/jit(_cho_solve)/triangular_solve/custom-call.4 | solution.py:66
  400.0 40.3 %all_to_all.20 = f32[128,1,2,1,128]{4,2,3,1,0:T(2,128)S(1)} all-to-all(f32[128,1,2,1,128]{4,2,3,1,0:T(2,128)S(1)} %constant_dynamic-update-slice_fusion.2), channel_id=1, replica_groups=mesh['energy'=128,'transpor'=4] {'energy'}, dimensions={0} | all-to-all | bytes 262144 | tf_op jit(solution)/shard_map/all_to_all | solution.py:205
  446.1 5.6 %all-to-all-start.1 = ((f32[128,2,1,128]{3,2,1,0:T(1,128)}), f32[128,2,1,128]{3,2,1,0:T(1,128)S(1)}, u32[]{:S(2)}, u32[]{:S(2)}) async-start(f32[128,2,1,128]{3,2,1,0:T(1,128)} %copy.299), calls=%async_computation.1 | async-start | bytes 262144 | tf_op jit(solution)/shard_map/all_to_all | solution.py:211
  452.3 12.2 %all-to-all-done.1 = f32[128,2,1,128]{3,2,1,0:T(1,128)S(1)} async-done(((f32[128,2,1,128]{3,2,1,0:T(1,128)}), f32[128,2,1,128]{3,2,1,0:T(1,128)S(1)}, u32[]{:S(2)}, u32[]{:S(2)}) %all-to-all-start.1) | async-done | bytes 131104 | tf_op jit(solution)/shard_map/all_to_all | solution.py:211
  (406 shorter events, 59.2 us)
Async XLA Ops:
  0.6 1.0 copy-start.1
  1.8 0.8 copy-start
  2.0 0.7 copy-start.2
  446.1 18.4 %all-to-all-start.1 = ((f32[128,2,1,128]{3,2,1,0:T(1,128)}), f32[128,2,1,128]{3,2,1,0:T(1,128)S(1)}, u32[]{:S(2)}, u32[]{:S(2)}) async-start(f32[128,2,1,128]{3,2,1,0:T(1,128)} %copy.299), calls=%async_computation.1 | async-start | bytes 262144 | tf_op jit(solution)/shard_map/all_to_all | solution.py:211
